TPU v7x, 32 devices: a whole 2x2x4 slice. The times are simulated.
32 devices in a mesh: ctx: 8 (over z, y), grp: 4 (over x, core).
Axes of the slice: x: 2, y: 2, z: 4, core: 2. Of those that a mesh axis runs over, the one named last changes fastest.
Arguments:
- channels: bfloat16 [4096, 5120], P(('ctx', 'grp')), may hold values from -6 to 6
- gates: bfloat16 [4096, 5120], P(('ctx', 'grp')), may hold values from -6 to 6
- b_proj: bfloat16 [4096, 128], P(('ctx', 'grp')), may hold values from -6 to 6
- c_proj: bfloat16 [4096, 128], P(('ctx', 'grp')), may hold values from -0.5 to 0.5
- step_size: bfloat16 [4096, 80], P(('ctx', 'grp')), may hold values from 0.001 to 1, as said below
- log_decay: bfloat16 [4096, 80], P(('ctx', 'grp')), may hold values from -1 to 0, as said below
- skip_gain: float32 [80], P('grp'), may hold values from 0.5 to 2
- norm_gain: float32 [5120], P('grp'), may hold values from 0.1 to 1.9
- out_weight: bfloat16 [5120, 2560], P('grp'), may hold values from -0.078125 to 0.078125
Outputs:
- layer_out: bfloat16 [4096, 2560], P(('ctx', 'grp'))
Inputs may be any that keep to these rules, and one draw needn't show every extreme that they name: `step_size`: each token's step of each head is positive. `log_decay`: each token's log decay of each head is negative.
All inputs are finite; a program needn't handle non-finite values.
Results may differ from a plain program's by a relative error of at most 0.009.
Values may be sent and summed in bfloat16 or wider, within the bound.
A program may use at most 128 MiB of HBM per device.

v0:
```python
import jax
import jax.numpy as jnp
from jax import lax
from jax.sharding import PartitionSpec as P

HEADS = 80
HD = 64
NSTATE = 128
GROUP = 256


def prefix_2(value, axis, join, neutral):
    count, mine = (lax.axis_size(axis), lax.axis_index(axis))
    pieces = jax.tree.map(lambda part: lax.all_gather(part, axis), value)
    so_far = jax.tree.map(
        lambda part, zero: jnp.full_like(part, 0) + jnp.asarray(zero, part.dtype), value, neutral
    )

    def turn(position, so_far):
        longer = join(so_far, jax.tree.map(lambda part: part[position], pieces))
        return jax.tree.map(lambda new, old: jnp.where(position < mine, new, old), longer, so_far)

    return lax.fori_loop(0, count - 1, turn, so_far)


def local_scan(chan_heads, step_heads, decay_heads, b_rows, c_rows):
    highest = lax.Precision.HIGHEST
    piece_len = chan_heads.shape[0]
    nheads = step_heads.shape[1]
    blocks = piece_len // GROUP
    running = jnp.cumsum(decay_heads.astype(jnp.float32).reshape(blocks, GROUP, nheads), axis=1)
    running_t = jnp.transpose(running, (0, 2, 1))
    chan_f = chan_heads.astype(jnp.float32).reshape(piece_len, nheads, HD)
    inputs = (chan_f * step_heads.astype(jnp.float32)[:, :, None]).reshape(
        blocks, GROUP, nheads, HD
    )
    b_blocks = b_rows.reshape(blocks, GROUP, NSTATE)
    c_blocks = c_rows.reshape(blocks, GROUP, NSTATE)
    scores = jnp.einsum("qin,qjn->qij", c_blocks, b_blocks, preferred_element_type=jnp.float32)
    rows_at = lax.broadcasted_iota(jnp.int32, (GROUP, GROUP), 0)
    cols_at = lax.broadcasted_iota(jnp.int32, (GROUP, GROUP), 1)
    causal = rows_at >= cols_at
    spread = running_t[:, :, :, None] - running_t[:, :, None, :]
    weights = jnp.where(causal[None, None], jnp.exp(spread), 0.0) * scores[:, None]
    y_intra = jnp.einsum("qhij,qjhp->qihp", weights, inputs, precision=highest)
    tail_decay = jnp.exp(running[:, -1:, :] - running)
    b_float = b_blocks.astype(jnp.float32)
    c_float = c_blocks.astype(jnp.float32)
    group_states = jnp.einsum(
        "qjhp,qjn->qhpn", inputs * tail_decay[..., None], b_float, precision=highest
    )
    totals = jnp.exp(running[:, -1, :])

    def carry_step(carried, packed):
        factor, fresh_state = packed
        return (factor[:, None, None] * carried + fresh_state, carried)

    final_state, starts = lax.scan(
        carry_step, jnp.zeros((nheads, HD, NSTATE), jnp.float32), (totals, group_states)
    )
    y_inter = (
        jnp.einsum("qin,qhpn->qihp", c_float, starts, precision=highest)
        * jnp.exp(running)[..., None]
    )
    group_logs = running[:, -1, :]
    offsets = jnp.cumsum(group_logs, axis=0) - group_logs
    piece_cum = (running + offsets[:, None, :]).reshape(piece_len, nheads)
    piece_log = jnp.sum(group_logs, axis=0)
    local_out = (y_intra + y_inter).reshape(piece_len, nheads, HD)
    return (local_out, final_state, piece_log, piece_cum, chan_f)


def local(channels, gates, b_proj, c_proj, step_size, log_decay, skip_gain, norm_gain, out_weight):
    highest = lax.Precision.HIGHEST
    chan_heads, gate_heads, step_heads, decay_heads = (
        lax.all_to_all(channels, "grp", split_axis=1, concat_axis=0, tiled=True),
        lax.all_to_all(gates, "grp", split_axis=1, concat_axis=0, tiled=True),
        lax.all_to_all(step_size, "grp", split_axis=1, concat_axis=0, tiled=True),
        lax.all_to_all(log_decay, "grp", split_axis=1, concat_axis=0, tiled=True),
    )
    b_rows, c_rows = (
        lax.all_gather(b_proj, "grp", axis=0, tiled=True),
        lax.all_gather(c_proj, "grp", axis=0, tiled=True),
    )
    local_out, final_state, piece_log, piece_cum, chan_f = local_scan(
        chan_heads, step_heads, decay_heads, b_rows, c_rows
    )
    piece_factor = jnp.exp(piece_log)

    def combine(early_part, later_part):
        return (
            early_part[0] * later_part[0],
            later_part[0][:, None, None] * early_part[1] + later_part[1],
        )

    identity = (jnp.ones_like(piece_factor), jnp.zeros_like(final_state))
    prefix = prefix_2((piece_factor, final_state), "ctx", combine, identity)
    incoming = prefix[1]
    correction = jnp.einsum("tn,hpn->thp", c_rows.astype(jnp.float32), incoming, precision=highest)
    correction = correction * jnp.exp(piece_cum)[:, :, None]
    ssm_out = local_out + correction + skip_gain[None, :, None] * chan_f
    piece_len = chan_heads.shape[0]
    gated_out = ssm_out.reshape(piece_len, chan_heads.shape[1]) * jax.nn.silu(
        gate_heads.astype(jnp.float32)
    )
    row_squares = lax.psum(jnp.sum(gated_out * gated_out, axis=1), "grp")
    scale = lax.rsqrt(row_squares / (HEADS * HD) + 1e-05)
    normed = (gated_out * scale[:, None] * norm_gain[None, :]).astype(jnp.bfloat16)
    return lax.psum_scatter(
        jnp.dot(normed, out_weight, preferred_element_type=jnp.float32).astype(jnp.bfloat16),
        "grp",
        scatter_dimension=0,
        tiled=True,
    )


def solution(mesh):
    in_specs = (
        P(("ctx", "grp"), None),
        P(("ctx", "grp"), None),
        P(("ctx", "grp"), None),
        P(("ctx", "grp"), None),
        P(("ctx", "grp"), None),
        P(("ctx", "grp"), None),
        P("grp"),
        P("grp"),
        P("grp", None),
    )
    out_specs = P(("ctx", "grp"), None)
    return jax.shard_map(local, mesh=mesh, in_specs=in_specs, out_specs=out_specs, check_vma=False)
```

profile of v0, /device:TPU:0, one launch (start us, length us, event | category | flops | bytes accessed | tf_op | source)
XLA Modules:
  0.0 233.1 jit_solution(6459703165636211416)
XLA Ops:
  6.5 1.4 all_to_all.44
  7.9 4.2 %all-to-all-start.2 = ((bf16[128,4,20]{0,2,1:T(8,128)(2,1)}), bf16[128,4,20]{0,2,1:T(8,128)(2,1)S(1)}, u32[]{:S(2)}, u32[]{:S(2)}) async-start(bf16[128,4,20]{0,2,1:T(8,128)(2,1)} %all_to_all.44), calls=%async_computation.2 | async-start | bytes 49152 | tf_op jit(solution)/shard_map/all_to_all | solution.py:79
  12.1 5.8 %all_gather.17 = bf16[512,128]{1,0:T(8,128)(2,1)S(1)} all-gather(bf16[128,128]{1,0:T(8,128)(2,1)} %param.15), channel_id=1, replica_groups=mesh['ctx'=8,'grp'=4] {'grp'}, dimensions={0}, use_global_device_ids=true | all-gather | bytes 163840 | tf_op jit(solution)/shard_map/all_gather | solution.py:82
  17.9 2.4 %copy.51 = bf16[128,5120]{0,1:T(8,128)(2,1)} copy(bf16[128,5120]{1,0:T(8,128)(2,1)} %param.13) | data formatting | bytes 2621440 | tf_op args[0]
  20.3 0.6 all_to_all.42
  20.9 3.3 %all-to-all-start.1 = ((bf16[128,4,20]{0,2,1:T(8,128)(2,1)}), bf16[128,4,20]{0,2,1:T(8,128)(2,1)S(1)}, u32[]{:S(2)}, u32[]{:S(2)}) async-start(bf16[128,4,20]{0,2,1:T(8,128)(2,1)} %all_to_all.42), calls=%async_computation.1 | async-start | bytes 49152 | tf_op jit(solution)/shard_map/all_to_all | solution.py:78
  24.3 1.2 reduce-window.6
  25.5 0.2 slice_reduce_fusion
  25.7 2.3 %all-to-all-done.1 = bf16[128,4,20]{0,2,1:T(8,128)(2,1)S(1)} async-done(((bf16[128,4,20]{0,2,1:T(8,128)(2,1)}), bf16[128,4,20]{0,2,1:T(8,128)(2,1)S(1)}, u32[]{:S(2)}, u32[]{:S(2)}) %all-to-all-start.1) | async-done | bytes 20512 | tf_op jit(solution)/shard_map/all_to_all | solution.py:78
  28.1 3.5 %all-to-all-start = ((bf16[128,4,1280]{0,2,1:T(8,128)(2,1)}), bf16[128,4,1280]{0,2,1:T(8,128)(2,1)S(1)}, u32[]{:S(2)}, u32[]{:S(2)}) async-start(bf16[128,4,1280]{0,2,1:T(8,128)(2,1)} %bitcast), calls=%async_computation | async-start | bytes 2621440 | tf_op jit(solution)/shard_map/all_to_all | solution.py:76
  32.0 0.1 copy.60
  32.1 0.3 slice_subtract_fusion
  32.4 0.1 copy.65
  32.5 0.1 copy.66
  32.6 0.1 copy.61
  32.8 0.7 exponential_bitcast_fusion
  33.5 15.3 %all-to-all-done = bf16[128,4,1280]{0,2,1:T(8,128)(2,1)S(1)} async-done(((bf16[128,4,1280]{0,2,1:T(8,128)(2,1)}), bf16[128,4,1280]{0,2,1:T(8,128)(2,1)S(1)}, u32[]{:S(2)}, u32[]{:S(2)}) %all-to-all-start) | async-done | bytes 1310752 | tf_op jit(solution)/shard_map/all_to_all | solution.py:76
  48.8 0.2 convert_bitcast_fusion.1
  49.0 5.4 %copy.52 = f32[4,128,1280]{1,0,2:T(4,128)S(1)} copy(f32[4,128,1280]{1,2,0:T(8,128)S(1)} %convert_bitcast_fusion.1) | data formatting | bytes 5242880 | tf_op jit(solution)/shard_map/convert_element_type | solution.py:33
  54.5 3.3 %reshape.122 = f32[2,256,20,64]{1,0,3,2:T(2,128)} reshape(f32[4,128,1280]{1,0,2:T(4,128)S(1)} %copy.52) | data formatting | bytes 5242880 | tf_op jit(solution)/shard_map/convert_element_type | solution.py:33
  57.8 5.1 %broadcast_multiply_fusion = (f32[2,256,20,64]{1,0,3,2:T(2,128)S(1)}, f32[2,256,20,64]{1,0,3,2:T(2,128)}) fusion(f32[2,256,20]{1,0,2:T(2,128)S(1)} %get-tuple-element.189, f32[2,256,20,64]{1,0,3,2:T(2,128)} %reshape.122, f32[2,256,20]{1,0,2:T(2,128)S(1)} %reshape.123), kind=kLoop, calls=%fused_computation.39 | loop fusion | flops 1310720 | bytes 7946240 | tf_op jit(solution)/shard_map/mul | solution.py:50
  62.9 2.4 %fusion.22 = f32[2,20,64,128]{3,2,1,0:T(8,128)} fusion(bf16[2,256,128,1]{2,1,3,0:T(8,128)(2,1)S(1)} %bitcast.131, f32[2,256,20,64]{1,0,3,2:T(2,128)S(1)} %get-tuple-element.186), kind=kOutput, calls=%fused_computation.33 | convolution fusion | flops 1006632960 | bytes 4063232 | tf_op jit(solution)/shard_map/qjhp,qjn->qhpn/dot_general | solution.py:49
  65.3 4.3 %while.27 = (s32[]{:T(128)}, f32[20,64,128]{2,1,0:T(8,128)S(1)}, f32[2,20,64,128]{3,2,1,0:T(8,128)}, f32[2,20]{1,0:T(2,128)S(1)}, f32[2,20,64,128]{3,2,1,0:T(8,128)}, /*index=5*/s32[]{:T(128)}, s32[]{:T(128)}) while((s32[]{:T(128)}, f32[20,64,128]{2,1,0:T(8,128)S(1)}, f32[2,20,64,128]{3,2,1,0:T(8,128)}, f32[2,20]{1,0:T(2,128)S(1)}, ...), condition=%wide.region_3.4_spmd.clone, body=%wide.region_2.3_spmd.clone.sunk | while | flops 655363 | bytes 3277648 | solution.py:58
  65.3 0.9 bitcast_dynamic-update-slice_fusion.2
  66.2 1.2 bitcast_add_fusion.3
  67.5 0.9 bitcast_dynamic-update-slice_fusion.2
  68.4 1.2 bitcast_add_fusion.3
  69.6 0.8 copy-done
  70.5 2.5 %copy.68 = bf16[128,5120]{0,1:T(8,128)(2,1)} copy(bf16[128,5120]{1,0:T(8,128)(2,1)} %param.14) | data formatting | bytes 2621440 | tf_op args[1]
  72.9 4.3 %all-to-all-start.3 = ((bf16[128,4,1280]{0,2,1:T(8,128)(2,1)}), bf16[128,4,1280]{0,2,1:T(8,128)(2,1)}, u32[]{:S(2)}, u32[]{:S(2)}) async-start(bf16[128,4,1280]{0,2,1:T(8,128)(2,1)} %bitcast.127), calls=%async_computation.3 | async-start | bytes 2621440 | tf_op jit(solution)/shard_map/all_to_all | solution.py:77
  77.4 0.6 dynamic-slice
  78.5 17.5 %all_gather.16 = bf16[512,128]{1,0:T(8,128)(2,1)S(1)} all-gather(bf16[128,128]{1,0:T(8,128)(2,1)} %param.16), channel_id=1, replica_groups=mesh['ctx'=8,'grp'=4] {'grp'}, dimensions={0}, use_global_device_ids=true | all-gather | bytes 163840 | tf_op jit(solution)/shard_map/all_gather | solution.py:83
  96.0 0.6 iota_compare_fusion
  96.7 1.0 fusion.28
  97.7 1.4 copy.57
  99.1 0.8 copy.63
  99.9 0.1 exponential_dynamic-update-slice_fusion
  100.0 22.7 %all-reduce = f32[160]{0:T(256)S(1)} all-reduce(f32[160]{0:T(256)S(1)} %exponential_dynamic-update-slice_fusion), channel_id=2, replica_groups=mesh['ctx'=8,'grp'=4] {'ctx'}, use_global_device_ids=true, to_apply=%add | all-reduce | flops 160 | bytes 1280
  122.7 0.1 reshape.129
  122.8 0.8 pad
  123.6 0.6 copy.75
  124.2 2.1 reshape.125
  126.3 13.1 %fusion.2 = f32[2,20,64,256]{3,2,1,0:T(8,128)S(1)} fusion(f32[2,256,256]{2,1,0:T(8,128)} %fusion.28, f32[2,20,256]{2,1,0:T(8,128)} %copy.57, pred[256,256]{1,0:T(8,128)(4,1)S(1)} %copy-done.3, f32[2,256,20,64]{1,0,3,2:T(2,128)} %get-tuple-element.187), kind=kOutput, calls=%fused_computation.7 | convolution fusion | flops 2021130240 | bytes 5873664 | tf_op jit(solution)/shard_map/qhij,qjhp->qihp/dot_general | solution.py:45
  139.5 1.3 fusion.21
  140.9 1.9 copy.74
  142.7 1.6 copy.69
  144.3 1.7 convert_bitcast_fusion
  146.1 4.1 %copy.71 = f32[4,128,1280]{1,0,2:T(4,128)} copy(f32[4,128,1280]{2,1,0:T(8,128)} %convert_bitcast_fusion) | data formatting | bytes 5242880 | tf_op jit(solution)/shard_map/convert_element_type | solution.py:104
  150.2 4.1 %reshape.127 = f32[512,20,64]{0,2,1:T(8,128)} reshape(f32[4,128,1280]{1,0,2:T(4,128)} %copy.71) | data formatting | bytes 5242880 | tf_op jit(solution)/shard_map/convert_element_type | solution.py:104
  154.4 3.5 %all-gather.4.cloned.1.call-done = f32[160,64,128]{2,1,0:T(8,128)} async-done(((f32[20,64,128]{2,1,0:T(8,128)}), f32[160,64,128]{2,1,0:T(8,128)}) %all-gather.4.cloned.1.call-update) | async-done | bytes 5242896 | tf_op jit(solution)/shard_map/all_gather | solution.py:14
  157.9 8.9 %while.28 = (s32[]{:T(128)}, f32[20,64,128]{2,1,0:T(8,128)S(1)}, s32[]{:T(128)}, f32[8,20]{1,0:T(8,128)S(1)}, f32[8,20,64,128]{3,2,1,0:T(8,128)}, /*index=5*/s32[]{:T(128)}, s32[]{:T(128)}) while((s32[]{:T(128)}, f32[20,64,128]{2,1,0:T(8,128)S(1)}, s32[]{:T(128)}, f32[8,20]{1,0:T(8,128)S(1)}, f32[8,20,64,128]{3,2,1,0:T(8,128)}, ...), condition=%wide.region_6.7_spmd.clone, body=%wide.region_5.6_spmd.clone.sunk | while | flops 655364 | bytes 1966425 | solution.py:23
  157.9 1.2 fusion.40
  159.2 1.2 fusion.40
  160.5 1.2 fusion.40
  161.7 1.2 fusion.40
  163.0 1.2 fusion.40
  164.3 1.2 fusion.40
  165.6 1.2 fusion.40
  166.8 6.9 %multiply_reduce_fusion = (f32[512]{0:T(512)S(1)}, f32[512,20,64]{0,2,1:T(8,128)}) fusion(f32[512,20,64]{0,2,1:T(8,128)} %reshape.127, f32[512,20,64]{0,2,1:T(8,128)} %reshape.125, f32[20]{0:T(128)S(1)} %copy-done.7, f32[512,20,64]{0,2,1:T(8,128)} %bitcast.128, f32[512,20]{0,1:T(8,128)S(1)} %bitcast.139, f32[20,64,128]{2,1,0:T(8,128)S(1)} %get-tuple-element.129, ...), kind=kOutput, calls=%fused_computation.37 | convolution fusion | flops 1013841408 | bytes 11315280 | tf_op jit(solution)/shard_map/tn,hpn->thp/dot_general | solution.py:99
  173.7 3.2 %copy.70 = f32[512,1280]{1,0:T(8,128)} copy(f32[512,1280]{0,1:T(8,128)} %bitcast.129) | data formatting | bytes 5242880 | tf_op jit(solution)/shard_map/reshape | solution.py:103
  176.9 5.9 %psum.7 = f32[512]{0:T(512)S(1)} all-reduce(f32[512]{0:T(512)S(1)} %get-tuple-element.193), channel_id=1, replica_groups=mesh['ctx'=8,'grp'=4] {'grp'}, use_global_device_ids=true, to_apply=%region_9.10 | all-reduce | flops 512 | bytes 4096 | tf_op jit(solution)/shard_map/psum | solution.py:106
  182.9 2.6 %fusion.25 = bf16[512,1280]{1,0:T(8,128)(2,1)S(1)} fusion(f32[512,1280]{1,0:T(8,128)} %copy.70, bf16[128,4,1280]{2,0,1:T(8,128)(2,1)S(1)} %copy.69, f32[1280]{0:T(1024)S(1)} %copy-done.6, f32[512]{0:T(512)S(1)} %add_rsqrt_fusion), kind=kLoop, calls=%fused_computation.38 | loop fusion | flops 5898240 | bytes 5250048 | tf_op jit(solution)/shard_map/convert_element_type | solution.py:108
  185.5 7.7 %convolution_convert_fusion = bf16[512,2560]{1,0:T(8,128)(2,1)} fusion(bf16[512,1280]{1,0:T(8,128)(2,1)S(1)} %fusion.25, bf16[1280,2560]{1,0:T(8,128)(2,1)} %param.21), kind=kOutput, calls=%fused_computation.17 | convolution fusion | flops 3356753920 | bytes 10485760 | tf_op jit(solution)/shard_map/dot_general | solution.py:110
  193.2 33.1 %reduce-scatter.2.cloned.1.call-done = bf16[128,2560]{1,0:T(8,128)(2,1)} async-done(((bf16[512,2560]{1,0:T(8,128)(2,1)}), bf16[128,2560]{1,0:T(8,128)(2,1)}) %reduce-scatter.2.cloned.1.call-update) | async-done | bytes 655376 | tf_op jit(solution)/shard_map/reduce_scatter | solution.py:109
  (53 shorter events, 0.7 us)
Async XLA Ops:
  6.5 13.8 %copy-start.5 = (bf16[128,80]{0,1:T(8,128)(2,1)S(1)}, bf16[128,80]{0,1:T(8,128)(2,1)}, u32[]{:S(2)}) copy-start(bf16[128,80]{0,1:T(8,128)(2,1)} %param.17) | copy-start | bytes 61444
  7.9 13.0 %all-to-all-start.2 = ((bf16[128,4,20]{0,2,1:T(8,128)(2,1)}), bf16[128,4,20]{0,2,1:T(8,128)(2,1)S(1)}, u32[]{:S(2)}, u32[]{:S(2)}) async-start(bf16[128,4,20]{0,2,1:T(8,128)(2,1)} %all_to_all.44), calls=%async_computation.2 | async-start | bytes 49152 | tf_op jit(solution)/shard_map/all_to_all | solution.py:79
  20.9 7.1 %all-to-all-start.1 = ((bf16[128,4,20]{0,2,1:T(8,128)(2,1)}), bf16[128,4,20]{0,2,1:T(8,128)(2,1)S(1)}, u32[]{:S(2)}, u32[]{:S(2)}) async-start(bf16[128,4,20]{0,2,1:T(8,128)(2,1)} %all_to_all.42), calls=%async_computation.1 | async-start | bytes 49152 | tf_op jit(solution)/shard_map/all_to_all | solution.py:78
  28.1 20.8 %all-to-all-start = ((bf16[128,4,1280]{0,2,1:T(8,128)(2,1)}), bf16[128,4,1280]{0,2,1:T(8,128)(2,1)S(1)}, u32[]{:S(2)}, u32[]{:S(2)}) async-start(bf16[128,4,1280]{0,2,1:T(8,128)(2,1)} %bitcast), calls=%async_computation | async-start | bytes 2621440 | tf_op jit(solution)/shard_map/all_to_all | solution.py:76
  31.6 126.3 %all-gather.4.cloned.1.call-start = ((), (), s32[]{:S(2)}) async-start(), calls=%async_computation.6 | async-start | bytes 5898240 | tf_op jit(solution)/shard_map/all_gather | solution.py:14
  31.8 17.0 %copy-start.2 = (f32[2,20,256]{2,0,1:T(2,128)}, f32[2,20,256]{2,0,1:T(2,128)S(1)}, u32[]{:S(2)}) copy-start(f32[2,20,256]{2,0,1:T(2,128)S(1)} %reduce_window_sum.35) | copy-start | bytes 122884
  69.6 0.8 copy-start
  70.5 6.9 %copy-start.8 = (u32[32]{0:T(128)S(1)}, u32[32]{0:T(128)}, u32[]{:S(2)}) copy-start(u32[32]{0:T(128)} %constant.61) | copy-start | bytes 388
  72.9 69.8 %all-to-all-start.3 = ((bf16[128,4,1280]{0,2,1:T(8,128)(2,1)}), bf16[128,4,1280]{0,2,1:T(8,128)(2,1)}, u32[]{:S(2)}, u32[]{:S(2)}) async-start(bf16[128,4,1280]{0,2,1:T(8,128)(2,1)} %bitcast.127), calls=%async_computation.3 | async-start | bytes 2621440 | tf_op jit(solution)/shard_map/all_to_all | solution.py:77
  77.3 149.0 %reduce-scatter.2.cloned.1.call-start = ((), (), s32[]{:S(2)}) async-start(), calls=%async_computation.5 | async-start | bytes 3276800 | tf_op jit(solution)/shard_map/reduce_scatter | solution.py:109
  124.2 2.1 copy-start.3
  126.3 13.1 %copy-start.1 = (f32[2,20,64,128]{3,2,1,0:T(8,128)S(1)}, f32[2,20,64,128]{3,2,1,0:T(8,128)}, u32[]{:S(2)}) copy-start(f32[2,20,64,128]{3,2,1,0:T(8,128)} %get-tuple-element.127) | copy-start | bytes 3932164
  157.9 8.9 %copy-start.4 = (f32[3,8,2,256]{3,1,2,0:T(8,128)S(1)}, f32[3,8,2,256]{3,1,2,0:T(8,128)}, u32[]{:S(2)}) copy-start(f32[3,8,2,256]{3,1,2,0:T(8,128)} %copy.75) | copy-start | bytes 147460
  157.9 8.9 %copy-start.7 = (f32[20]{0:T(128)S(1)}, f32[20]{0:T(128)}, u32[]{:S(2)}) copy-start(f32[20]{0:T(128)} %param.19) | copy-start | bytes 244
  173.7 9.2 %copy-start.6 = (f32[1280]{0:T(1024)S(1)}, f32[1280]{0:T(1024)}, u32[]{:S(2)}) copy-start(f32[1280]{0:T(1024)} %param.20) | copy-start | bytes 15364
Sparse Core Ops, SparseCore 0:
  70.6 87.2 all-gather.3
  193.3 32.9 reduce-scatter.1
where the time goes:
time: 235 us; the launch traced here: 233 us
  waiting for transfers between devices  54.3 us (23%)
  blocking collectives  51.9 us (22%)
  local copies, waits for them, and re-layouts  38.9 us (17%)
  matrix products  32.5 us (14%)
  other arithmetic  25.6 us (11%)
  starting transfers between devices  15.4 us (7%)
  between operations  14.3 us (6%)
    reduce_scatter x1, waiting for transfers between devices, local(): lax.psum_scatter(jnp.dot(normed, out_weight, preferred_element_type=jnp.f...  33.1 us
    unnamed x1, blocking collectives  22.7 us
    all_gather x1, blocking collectives, local(): lax.all_gather(c_proj, 'grp', axis=0, tiled=True)  17.5 us
    all_to_all x1, waiting for transfers between devices, local(): lax.all_to_all(channels, 'grp', split_axis=1, concat_axis=0, tiled=True)  15.3 us
    dot_general x1, matrix products, local_scan(): y_intra = jnp.einsum('qhij,qjhp->qihp', weights, inputs, precision=highest)  13.1 us
    convert_element_type x3, local copies, waits for them, and re-layouts, local_scan(): chan_f = chan_heads.astype(jnp.float32).reshape(piece_len, nheads, HD)  10.9 us
    select_n x7, other arithmetic, turn(): jnp.where(position < mine, new, old)  8.64 us
    convert_element_type x2, local copies, waits for them, and re-layouts, local(): gate_heads.astype(jnp.float32)  8.27 us
  transfers between devices with their start and end apart: 6, of which 4 were waited for; matrix products, arithmetic and copies ran while one was open for 19% of the time, Pallas kernels for 0%

commit v1 on v0

v1 whole, which is shorter than its diff:
```python
import functools

import jax
import jax.numpy as jnp
from jax import lax
from jax.experimental import pallas as pl
from jax.experimental.pallas import tpu as pltpu
from jax.sharding import PartitionSpec as P

HD = 64
LANES = 128
COLS = 512
F32 = jnp.float32
BF16 = jnp.bfloat16
MESH_ID = pl.DeviceIdType.MESH


def dot(a, b):
    return jnp.dot(a, b, preferred_element_type=F32)


def layer_kernel(
    n_ctx,
    n_grp,
    inner,
    chan_ref,
    gate_ref,
    bc_ref,
    sd_ref,
    skip_ref,
    gain_ref,
    w_ref,
    out_ref,
    chan_all,
    gate_all,
    bc_all,
    sd_all,
    w_all,
    b_t,
    scores,
    tail_w,
    total_e,
    y_acc,
    e_acc,
    z_all,
    s_start,
    d_start,
    s_fin,
    chain_out,
    chain_in,
    prod,
    sib_out,
    sib_in,
    far_out,
    far_in,
    own_acc,
    ssq_out,
    ssq_in,
    local_sem,
    chan_send,
    chan_recv,
    gate_send,
    gate_recv,
    bc_send,
    bc_recv,
    sd_send,
    sd_recv,
    chain_send,
    chain_recv,
    sib_send,
    sib_recv,
    far_send,
    far_recv,
    ssq_send,
    ssq_recv,
):
    ctx = lax.axis_index("ctx")
    me = lax.axis_index("grp")
    tok = chan_ref.shape[0]
    width = chan_all.shape[2]
    pairs = width // LANES
    n_chip = n_grp // 2
    chip = me // 2
    core = lax.rem(me, 2)
    sib = chip * 2 + 1 - core
    n_col = sib_out.shape[1]

    barrier = pltpu.get_barrier_semaphore()
    for off in range(1, n_grp):
        pl.semaphore_signal(
            barrier,
            inc=1,
            device_id={"grp": lax.rem(me + off, n_grp)},
            device_id_type=MESH_ID,
        )

    @pl.when(ctx > 0)
    def _():
        pl.semaphore_signal(barrier, inc=1, device_id={"ctx": ctx - 1}, device_id_type=MESH_ID)

    @pl.when(ctx < n_ctx - 1)
    def _():
        pl.semaphore_signal(barrier, inc=1, device_id={"ctx": ctx + 1}, device_id_type=MESH_ID)

    def columns(ref, where):
        return ref.at[:, pl.ds(pl.multiple_of(where * width, LANES), width)]

    own = [
        pltpu.make_async_copy(columns(chan_ref, me), chan_all.at[me], local_sem.at[0]),
        pltpu.make_async_copy(bc_ref, bc_all.at[me], local_sem.at[1]),
        pltpu.make_async_copy(sd_ref.at[me], sd_all.at[me], local_sem.at[2]),
        pltpu.make_async_copy(columns(gate_ref, me), gate_all.at[me], local_sem.at[3]),
        pltpu.make_async_copy(w_ref, w_all, local_sem.at[4]),
    ]
    for copy in own:
        copy.start()

    neighbours = jnp.where(ctx > 0, 1, 0) + jnp.where(ctx < n_ctx - 1, 1, 0)
    pl.semaphore_wait(barrier, n_grp - 1 + neighbours)

    def push(src, dst, send, recv, peer):
        return pltpu.make_async_remote_copy(
            src_ref=src,
            dst_ref=dst,
            send_sem=send,
            recv_sem=recv,
            device_id={"grp": peer},
            device_id_type=MESH_ID,
        )

    early, late = [], []
    for off in range(1, n_grp):
        peer = lax.rem(me + off, n_grp)
        early.append(push(bc_ref, bc_all.at[me], bc_send.at[off], bc_recv.at[off], peer))
        early.append(push(sd_ref.at[peer], sd_all.at[me], sd_send.at[off], sd_recv.at[off], peer))
    for off in range(1, n_grp):
        peer = lax.rem(me + off, n_grp)
        early.append(
            push(columns(chan_ref, peer), chan_all.at[me], chan_send.at[off], chan_recv.at[off], peer)
        )
        late.append(
            push(columns(gate_ref, peer), gate_all.at[me], gate_send.at[off], gate_recv.at[off], peer)
        )
    for copy in early + late:
        copy.start()

    rows = lax.broadcasted_iota(jnp.int32, (tok, tok), 0)
    cols = lax.broadcasted_iota(jnp.int32, (tok, tok), 1)
    causal = rows >= cols
    after = (rows > cols).astype(F32).astype(BF16)
    lane = lax.broadcasted_iota(jnp.int32, (tok, LANES), 1)
    first = lane < HD
    left = first.astype(F32).astype(BF16)
    right = (lane >= HD).astype(F32).astype(BF16)
    ones = jnp.ones((tok, LANES), BF16)
    after_left = jnp.concatenate([after, left], axis=1)
    after_right = jnp.concatenate([after, right], axis=1)
    after_ones = jnp.concatenate([after, ones], axis=1)

    for copy in own[:3]:
        copy.wait()
    for copy in early[: 2 * (n_grp - 1)]:
        copy.wait_recv()
    for q in range(n_grp):
        b_blk = bc_all[q, :, :LANES]
        c_blk = bc_all[q, :, LANES:]
        b_t[q] = jnp.transpose(b_blk.astype(F32))
        both = lax.dot_general(
            c_blk, b_blk, (((1,), (1,)), ((), ())), preferred_element_type=F32
        )
        scores[q] = jnp.where(causal, both, 0.0)
        sums = dot(sd_all[q, 1].astype(BF16), after_ones)
        tail_w[q] = jnp.exp(sums[:, :LANES]) * sd_all[q, 0]
        total_e[q] = jnp.exp(sums[:, LANES:])
    for copy in early[2 * (n_grp - 1) :]:
        copy.wait_recv()

    first_row = first[:1]

    def lanes_of(pair):
        return pl.ds(pl.multiple_of(pair * LANES, LANES), LANES)

    def state_pair(pair, carry):
        state = jnp.zeros((LANES, LANES), F32)
        decay = jnp.ones((1, LANES), F32)
        for q in range(n_grp):
            s_start[q, pair] = state
            d_start[q, pl.ds(pair, 1), :] = decay
            x = chan_all[q, :, lanes_of(pair)]
            b_q = b_t[q]
            b0 = (b_q * tail_w[q, pl.ds(2 * pair, 1), :]).astype(BF16)
            b1 = (b_q * tail_w[q, pl.ds(2 * pair + 1, 1), :]).astype(BF16)
            fresh = dot(
                jnp.concatenate([b0, b1], axis=1), jnp.concatenate([x * left, x * right], axis=0)
            )
            total = jnp.where(
                first_row,
                total_e[q, pl.ds(2 * pair, 1), :],
                total_e[q, pl.ds(2 * pair + 1, 1), :],
            )
            state = state * total + fresh
            decay = decay * total
        s_fin[pair] = state
        d_start[n_grp, pl.ds(pair, 1), :] = decay
        return carry

    lax.fori_loop(0, pairs, state_pair, 0)

    def hop(pair):
        return pltpu.make_async_remote_copy(
            src_ref=chain_out.at[pair],
            dst_ref=chain_in.at[pair],
            send_sem=chain_send.at[pair],
            recv_sem=chain_recv.at[pair],
            device_id={"ctx": lax.rem(ctx + 1, n_ctx)},
            device_id_type=MESH_ID,
        )

    def chain_pair(pair):
        @pl.when(ctx == 0)
        def _():
            chain_in[pair] = jnp.zeros((LANES, LANES), chain_in.dtype)

        @pl.when(ctx > 0)
        def _():
            hop(pair).wait_recv()

        @pl.when(ctx < n_ctx - 1)
        def _():
            total = chain_in[pair].astype(F32) * d_start[n_grp, pl.ds(pair, 1), :] + s_fin[pair]
            chain_out[pair] = total.astype(chain_out.dtype)
            hop(pair).start()

    def within_pair(pair):
        at = lanes_of(pair)
        skip = skip_ref[:, at]
        for q in range(n_grp):
            x = chan_all[q, :, at]
            d0 = jnp.where(causal, sd_all[q, 1, pl.ds(2 * pair, 1), :], 0.0).astype(BF16)
            d1 = jnp.where(causal, sd_all[q, 1, pl.ds(2 * pair + 1, 1), :], 0.0).astype(BF16)
            r0 = dot(d0, after_left)
            r1 = dot(d1, after_right)
            sc = scores[q]
            w0 = jnp.exp(r0[:, :LANES]) * (sc * sd_all[q, 0, pl.ds(2 * pair, 1), :])
            w1 = jnp.exp(r1[:, :LANES]) * (sc * sd_all[q, 0, pl.ds(2 * pair + 1, 1), :])
            e_acc[q, :, at] = jnp.exp(r0[:, LANES:] + r1[:, LANES:])
            weights = jnp.concatenate([w0.astype(BF16), w1.astype(BF16)], axis=1)
            y = dot(weights, jnp.concatenate([x * left, x * right], axis=0))
            y_acc[q, :, at] = y + skip * x.astype(F32)

    lag = jnp.minimum(ctx, pairs)

    def mixed(step, carry):
        @pl.when(step < pairs)
        def _():
            within_pair(step)

        @pl.when((step >= lag) & (step < lag + pairs))
        def _():
            chain_pair(step - lag)

        return carry

    lax.fori_loop(0, 2 * pairs, mixed, 0)

    own[3].wait()
    for copy in late:
        copy.wait_recv()
    own[4].wait()

    ssq_copies = {}
    for turn in range(1, n_chip + 1):
        chip_to = lax.rem(chip + turn, n_chip)

        def gate_pair(pair, sums, chip_to=chip_to):
            at = lanes_of(pair)
            arrived = chain_in[pair].astype(F32)
            gain = gain_ref[:, at]
            res = []
            for c in range(2):
                q = chip_to * 2 + c
                state = s_start[q, pair] + d_start[q, pl.ds(pair, 1), :] * arrived
                y = y_acc[q, :, at] + e_acc[q, :, at] * dot(
                    bc_all[q, :, LANES:], state.astype(BF16)
                )
                g = gate_all[q, :, at].astype(F32)
                gated = y * (g / (1.0 + jnp.exp(-g)))
                res.append(sums[c] + gated * gated)
                z_all[chip_to, pl.ds(c * tok, tok), at] = (gated * gain).astype(BF16)
            return tuple(res)

        zero = jnp.zeros((tok, LANES), F32)
        sums = lax.fori_loop(0, pairs, gate_pair, (zero, zero))
        for c in range(2):
            row = jnp.sum(jnp.transpose(sums[c]), axis=0, keepdims=True)
            ssq_out[chip_to * 2 + c] = jnp.broadcast_to(row, (8, tok))
        for c in range(2):
            q = chip_to * 2 + c
            off = lax.rem(q - me + n_grp, n_grp)

            @pl.when(q != me)
            def _(q=q, off=off):
                push(
                    ssq_out.at[q], ssq_in.at[off], ssq_send.at[off], ssq_recv.at[off], q
                ).start()

        slot = turn - 1

        def to_sib(t, slot=slot):
            return push(
                sib_out.at[slot, t], sib_in.at[slot, t], sib_send.at[slot, t], sib_recv.at[slot, t], sib
            )

        def to_far(t, slot=slot, chip_to=chip_to):
            return push(
                far_out.at[slot, t],
                far_in.at[slot, t],
                far_send.at[slot, t],
                far_recv.at[slot, t],
                chip_to * 2 + core,
            )

        def project(t, carry, turn=turn, chip_to=chip_to, to_sib=to_sib, to_far=to_far, slot=slot):
            @pl.when(t < n_col)
            def _():
                at = pl.ds(pl.multiple_of(t * COLS, COLS), COLS)
                prod[lax.rem(t, 2)] = dot(z_all[chip_to], w_all[:, at])
                sib_out[slot, t] = prod[lax.rem(t, 2), pl.ds((1 - core) * tok, tok), :].astype(BF16)
                to_sib(t).start()

            @pl.when(t > 0)
            def _():
                mine = prod[lax.rem(t + 1, 2), pl.ds(core * tok, tok), :]
                to_sib(t - 1).wait_recv()
                both = mine + sib_in[slot, t - 1].astype(F32)
                if turn < n_chip:
                    far_out[slot, t - 1] = both.astype(BF16)
                    to_far(t - 1).start()
                else:
                    own_acc[t - 1] = both

            return carry

        lax.fori_loop(0, n_col + 1, project, 0)

    squares = ssq_out[me]
    for off in range(1, n_grp):
        copy = push(
            ssq_out.at[lax.rem(me + off, n_grp)],
            ssq_in.at[off],
            ssq_send.at[off],
            ssq_recv.at[off],
            lax.rem(me + off, n_grp),
        )
        copy.wait_recv()
        squares = squares + ssq_in[off]
    scale_row = lax.rsqrt(squares[:1] / inner + 1e-05)
    scale = jnp.transpose(jnp.broadcast_to(scale_row, (tok, tok)))

    def far_copy(slot, t):
        peer = lax.rem(chip + slot + 1, n_chip) * 2 + core
        return push(
            far_out.at[slot, t], far_in.at[slot, t], far_send.at[slot, t], far_recv.at[slot, t], peer
        )

    def finish(t, carry):
        total = own_acc[t]
        for slot in range(n_chip - 1):
            far_copy(slot, t).wait_recv()
            total = total + far_in[slot, t].astype(F32)
        for k in range(COLS // LANES):
            at = pl.ds(pl.multiple_of(t * COLS + k * LANES, LANES), LANES)
            out_ref[:, at] = (total[:, k * LANES : (k + 1) * LANES] * scale).astype(BF16)
        return carry

    lax.fori_loop(0, n_col, finish, 0)

    for copy in early + late:
        copy.wait_send()
    for off in range(1, n_grp):
        peer = lax.rem(me + off, n_grp)
        push(
            ssq_out.at[peer], ssq_in.at[off], ssq_send.at[off], ssq_recv.at[off], peer
        ).wait_send()

    @pl.when(ctx < n_ctx - 1)
    def _():
        def done(pair, carry):
            hop(pair).wait_send()
            return carry

        lax.fori_loop(0, pairs, done, 0)

    def sent(t, carry):
        for slot in range(n_chip):
            push(
                sib_out.at[slot, t], sib_in.at[slot, t], sib_send.at[slot, t], sib_recv.at[slot, t], sib
            ).wait_send()
        for slot in range(n_chip - 1):
            far_copy(slot, t).wait_send()
        return carry

    lax.fori_loop(0, n_col, sent, 0)


def local(
    n_ctx, n_grp, channels, gates, b_proj, c_proj, step_size, log_decay, skip_gain, norm_gain, out_weight
):
    tok, inner = channels.shape
    width, model = out_weight.shape
    heads = skip_gain.shape[0]
    pairs = width // LANES
    n_chip = n_grp // 2
    n_col = model // COLS
    bc = jnp.concatenate([b_proj, c_proj], axis=1)
    sd = jnp.stack(
        [
            jnp.transpose(step_size.astype(F32)).reshape(n_grp, heads, tok),
            jnp.transpose(log_decay.astype(F32)).reshape(n_grp, heads, tok),
        ],
        axis=1,
    )
    skip = jnp.repeat(skip_gain, HD).reshape(1, width)
    gain = norm_gain.reshape(1, width)
    hbm = pl.BlockSpec(memory_space=pl.ANY)
    vmem = pl.BlockSpec(memory_space=pltpu.VMEM)
    dma = pltpu.SemaphoreType.DMA
    return pl.pallas_call(
        functools.partial(layer_kernel, n_ctx, n_grp, inner),
        out_shape=jax.ShapeDtypeStruct((tok, model), BF16),
        in_specs=[hbm, hbm, hbm, hbm, vmem, vmem, hbm],
        out_specs=vmem,
        scratch_shapes=[
            pltpu.VMEM((n_grp, tok, width), BF16),
            pltpu.VMEM((n_grp, tok, width), BF16),
            pltpu.VMEM((n_grp, tok, 2 * LANES), BF16),
            pltpu.VMEM((n_grp, 2, heads, tok), F32),
            pltpu.VMEM((width, model), BF16),
            pltpu.VMEM((n_grp, LANES, tok), F32),
            pltpu.VMEM((n_grp, tok, tok), F32),
            pltpu.VMEM((n_grp, heads, LANES), F32),
            pltpu.VMEM((n_grp, heads, LANES), F32),
            pltpu.VMEM((n_grp, tok, width), F32),
            pltpu.VMEM((n_grp, tok, width), F32),
            pltpu.VMEM((n_chip, 2 * tok, width), BF16),
            pltpu.VMEM((n_grp, pairs, LANES, LANES), F32),
            pltpu.VMEM((n_grp + 1, pairs, LANES), F32),
            pltpu.VMEM((pairs, LANES, LANES), F32),
            pltpu.VMEM((pairs, LANES, LANES), BF16),
            pltpu.VMEM((pairs, LANES, LANES), BF16),
            pltpu.VMEM((2, 2 * tok, COLS), F32),
            pltpu.VMEM((n_chip, n_col, tok, COLS), BF16),
            pltpu.VMEM((n_chip, n_col, tok, COLS), BF16),
            pltpu.VMEM((n_chip - 1, n_col, tok, COLS), BF16),
            pltpu.VMEM((n_chip - 1, n_col, tok, COLS), BF16),
            pltpu.VMEM((n_col, tok, COLS), F32),
            pltpu.VMEM((n_grp, 8, tok), F32),
            pltpu.VMEM((n_grp, 8, tok), F32),
            dma((5,)),
            dma((n_grp,)),
            dma((n_grp,)),
            dma((n_grp,)),
            dma((n_grp,)),
            dma((n_grp,)),
            dma((n_grp,)),
            dma((n_grp,)),
            dma((n_grp,)),
            dma((pairs,)),
            dma((pairs,)),
            dma((n_chip, n_col)),
            dma((n_chip, n_col)),
            dma((n_chip - 1, n_col)),
            dma((n_chip - 1, n_col)),
            dma((n_grp,)),
            dma((n_grp,)),
        ],
        compiler_params=pltpu.CompilerParams(
            collective_id=0, has_side_effects=True, vmem_limit_bytes=52 << 20
        ),
        name="layer",
    )(channels, gates, bc, sd, skip, gain, out_weight)


def solution(mesh):
    in_specs = (
        P(("ctx", "grp"), None),
        P(("ctx", "grp"), None),
        P(("ctx", "grp"), None),
        P(("ctx", "grp"), None),
        P(("ctx", "grp"), None),
        P(("ctx", "grp"), None),
        P("grp"),
        P("grp"),
        P("grp", None),
    )
    out_specs = P(("ctx", "grp"), None)
    body = functools.partial(local, mesh.shape["ctx"], mesh.shape["grp"])
    return jax.shard_map(body, mesh=mesh, in_specs=in_specs, out_specs=out_specs, check_vma=False)
```

time: 235 us -> 72 us (0.31)
  the two profiles are of different devices: /device:TPU:0 before, /device:TPU:30 now
where the time goes in v1:
time: 72 us; the launch traced here: 71.6 us
  Pallas kernels  67 us (93%)
  local copies, waits for them, and re-layouts  3.81 us (5%)
  other arithmetic  0.8 us (1%)
    pallas_call x1, Pallas kernels, local(): pl.pallas_call(functools.partial(layer_kernel, n_ctx, n_grp, inner), out_...  67 us
    another operation x2, local copies, waits for them, and re-layouts, local(): jnp.stack([jnp.transpose(step_size.astype(F32)).reshape(n_grp, heads, tok...  1.47 us

profile of v1, /device:TPU:30, one launch (start us, length us, event | category | flops | bytes accessed | tf_op | source)
XLA Modules:
  0.0 71.6 jit_solution(3119283850975039400)
XLA Ops:
  0.0 0.7 reshape.3.gain_ref
  0.7 0.7 %broadcast_in_dim.3 = f32[20,64]{1,0:T(8,128)S(1)} broadcast(f32[20]{0:T(128)} %param.15), dimensions={0} | broadcast | bytes 5200 | tf_op jit(solution)/shard_map/broadcast_in_dim | solution.py:423
  1.4 0.1 reshape_reshape.3.skip_ref
  1.5 0.7 %stack_reshape.8 = bf16[4,1,20,128]{3,2,0,1:T(8,128)(2,1)S(1)} reshape(bf16[80,128]{1,0:T(8,128)(2,1)} %bitcast.6) | data formatting | bytes 40960 | tf_op jit(solution)/shard_map/stack;reshape | solution.py:416
  2.2 0.7 %stack_reshape.9 = bf16[4,1,20,128]{3,2,0,1:T(8,128)(2,1)S(1)} reshape(bf16[80,128]{1,0:T(8,128)(2,1)} %bitcast.7) | data formatting | bytes 40960 | tf_op jit(solution)/shard_map/stack;reshape | solution.py:416
  3.0 0.8 %pad_maximum_fusion.bc_ref = bf16[128,256]{1,0:T(8,128)(2,1)S(1)} fusion(bf16[128,128]{1,0:T(8,128)(2,1)} %param.12, bf16[128,128]{1,0:T(8,128)(2,1)} %param.11), kind=kLoop, calls=%fused_computation | loop fusion | flops 131072 | bytes 131072 | tf_op jit(solution)/shard_map/concatenate | solution.py:415
  3.8 67.0 %layer.1 = bf16[128,2560]{1,0:T(8,128)(2,1)S(1)} custom-call(bf16[128,5120]{1,0:T(8,128)(2,1)} %chan_ref.1, bf16[128,5120]{1,0:T(8,128)(2,1)} %gate_ref.1, bf16[128,256]{1,0:T(8,128)(2,1)S(1)} %pad_maximum_fusion.bc_ref, f32[4,2,20,128]{3,2,1,0:T(8,128)S(1)} %maximum_convert_fusion.sd_ref, f32[1,1280]{1,0:T(1,128)S(1)} %reshape_reshape.3.skip_ref, ...), custom_call_target="tpu_custom_call" | custom-call | tf_op jit(solution)/shard_map/layer/pallas_call | solution.py:428
  70.8 0.8 %copy.13 = bf16[128,2560]{1,0:T(8,128)(2,1)} copy(bf16[128,2560]{1,0:T(8,128)(2,1)S(1)} %layer.1) | data formatting | bytes 1310720
  (1 shorter events, 0.0 us)

commit v2 on v1

--- a/solution.py
+++ b/solution.py
@@ -25,15 +25,24 @@
     inner,
     chan_ref,
     gate_ref,
-    bc_ref,
-    sd_ref,
+    b_ref,
+    c_ref,
+    step_ref,
+    decay_ref,
     skip_ref,
     gain_ref,
     w_ref,
     out_ref,
     chan_all,
     gate_all,
-    bc_all,
+    step_raw,
+    decay_raw,
+    skip_raw,
+    gain_raw,
+    b_all,
+    c_all,
+    sd_out,
+    sd_in,
     sd_all,
     w_all,
     b_t,
@@ -46,6 +55,11 @@
     s_start,
     d_start,
     s_fin,
+    dec,
+    dec_in,
+    mate_out,
+    mate_in,
+    arrived_all,
     chain_out,
     chain_in,
     prod,
@@ -54,6 +68,7 @@
     far_out,
     far_in,
     own_acc,
+    gain_rows,
     ssq_out,
     ssq_in,
     local_sem,
@@ -61,10 +76,15 @@
     chan_recv,
     gate_send,
     gate_recv,
-    bc_send,
-    bc_recv,
+    b_send,
+    b_recv,
+    c_send,
+    c_recv,
     sd_send,
     sd_recv,
+    dec_sem,
+    mate_send,
+    mate_recv,
     chain_send,
     chain_recv,
     sib_send,
@@ -82,6 +102,10 @@
     n_chip = n_grp // 2
     chip = me // 2
     core = lax.rem(me, 2)
+    inner_ctx = lax.rem(ctx, 2)
+    outer = ctx // 2
+    n_out = n_ctx // 2
+    mate = ctx + 1 - 2 * inner_ctx
     sib = chip * 2 + 1 - core
     n_col = sib_out.shape[1]
 
@@ -94,29 +118,45 @@
             device_id_type=MESH_ID,
         )
 
-    @pl.when(ctx > 0)
+    pl.semaphore_signal(barrier, inc=1, device_id={"ctx": mate}, device_id_type=MESH_ID)
+
+    @pl.when(outer > 0)
     def _():
-        pl.semaphore_signal(barrier, inc=1, device_id={"ctx": ctx - 1}, device_id_type=MESH_ID)
-
-    @pl.when(ctx < n_ctx - 1)
+        pl.semaphore_signal(barrier, inc=1, device_id={"ctx": ctx - 2}, device_id_type=MESH_ID)
+
+    @pl.when(outer < n_out - 1)
     def _():
-        pl.semaphore_signal(barrier, inc=1, device_id={"ctx": ctx + 1}, device_id_type=MESH_ID)
+        pl.semaphore_signal(barrier, inc=1, device_id={"ctx": ctx + 2}, device_id_type=MESH_ID)
 
     def columns(ref, where):
         return ref.at[:, pl.ds(pl.multiple_of(where * width, LANES), width)]
 
     own = [
-        pltpu.make_async_copy(columns(chan_ref, me), chan_all.at[me], local_sem.at[0]),
-        pltpu.make_async_copy(bc_ref, bc_all.at[me], local_sem.at[1]),
-        pltpu.make_async_copy(sd_ref.at[me], sd_all.at[me], local_sem.at[2]),
-        pltpu.make_async_copy(columns(gate_ref, me), gate_all.at[me], local_sem.at[3]),
-        pltpu.make_async_copy(w_ref, w_all, local_sem.at[4]),
+        pltpu.make_async_copy(step_ref, step_raw, local_sem.at[0]),
+        pltpu.make_async_copy(decay_ref, decay_raw, local_sem.at[1]),
+        pltpu.make_async_copy(b_ref, b_all.at[me], local_sem.at[2]),
+        pltpu.make_async_copy(c_ref, c_all.at[me], local_sem.at[3]),
+        pltpu.make_async_copy(skip_ref, skip_raw, local_sem.at[4]),
+        pltpu.make_async_copy(gain_ref, gain_raw, local_sem.at[5]),
+        pltpu.make_async_copy(columns(chan_ref, me), chan_all.at[me], local_sem.at[6]),
+        pltpu.make_async_copy(columns(gate_ref, me), gate_all.at[me], local_sem.at[7]),
+        pltpu.make_async_copy(w_ref, w_all, local_sem.at[8]),
     ]
     for copy in own:
         copy.start()
-
-    neighbours = jnp.where(ctx > 0, 1, 0) + jnp.where(ctx < n_ctx - 1, 1, 0)
-    pl.semaphore_wait(barrier, n_grp - 1 + neighbours)
+    for copy in own[:2]:
+        copy.wait()
+    heads = step_raw.shape[0] // n_grp
+    padded = sd_all.shape[2]
+    taken = lax.broadcasted_iota(jnp.int32, (padded, n_grp * heads), 0)
+    given = lax.broadcasted_iota(jnp.int32, (padded, n_grp * heads), 1)
+    for peer in range(n_grp):
+        pick = (given == taken + peer * heads).astype(F32).astype(BF16)
+        sd_out[peer, 0] = dot(pick, step_raw[...]).astype(BF16)
+        sd_out[peer, 1] = dot(pick, decay_raw[...]).astype(BF16)
+
+    neighbours = jnp.where(outer > 0, 1, 0) + jnp.where(outer < n_out - 1, 1, 0)
+    pl.semaphore_wait(barrier, n_grp + neighbours)
 
     def push(src, dst, send, recv, peer):
         return pltpu.make_async_remote_copy(
@@ -128,21 +168,39 @@
             device_id_type=MESH_ID,
         )
 
-    early, late = [], []
+    small = []
     for off in range(1, n_grp):
         peer = lax.rem(me + off, n_grp)
-        early.append(push(bc_ref, bc_all.at[me], bc_send.at[off], bc_recv.at[off], peer))
-        early.append(push(sd_ref.at[peer], sd_all.at[me], sd_send.at[off], sd_recv.at[off], peer))
-    for off in range(1, n_grp):
+        small.append(push(b_ref, b_all.at[me], b_send.at[off], b_recv.at[off], peer))
+        small.append(push(c_ref, c_all.at[me], c_send.at[off], c_recv.at[off], peer))
+        small.append(push(sd_out.at[peer], sd_in.at[off], sd_send.at[off], sd_recv.at[off], peer))
+
+    n_part = chan_send.shape[0]
+    part_pairs = pairs // n_part
+    part_width = width // n_part
+
+    def col_part(src, dst, send, recv, part, off):
         peer = lax.rem(me + off, n_grp)
-        early.append(
-            push(columns(chan_ref, peer), chan_all.at[me], chan_send.at[off], chan_recv.at[off], peer)
-        )
-        late.append(
-            push(columns(gate_ref, peer), gate_all.at[me], gate_send.at[off], gate_recv.at[off], peer)
-        )
-    for copy in early + late:
+        begin = pl.multiple_of(part * part_width, LANES)
+        return push(
+            src.at[:, pl.ds(pl.multiple_of(peer * width + begin, LANES), part_width)],
+            dst.at[me, :, pl.ds(begin, part_width)],
+            send.at[part, off],
+            recv.at[part, off],
+            peer,
+        )
+
+    def chan_part(part, off):
+        return col_part(chan_ref, chan_all, chan_send, chan_recv, part, off)
+
+    def gate_part(part, off):
+        return col_part(gate_ref, gate_all, gate_send, gate_recv, part, off)
+
+    for copy in small:
         copy.start()
+    for part in range(n_part):
+        for off in range(1, n_grp):
+            chan_part(part, off).start()
 
     rows = lax.broadcasted_iota(jnp.int32, (tok, tok), 0)
     cols = lax.broadcasted_iota(jnp.int32, (tok, tok), 1)
@@ -157,30 +215,59 @@
     after_right = jnp.concatenate([after, right], axis=1)
     after_ones = jnp.concatenate([after, ones], axis=1)
 
-    for copy in own[:3]:
+    for copy in own[2:7]:
         copy.wait()
-    for copy in early[: 2 * (n_grp - 1)]:
+    for pair in range(pairs):
+        gain_rows[pair : pair + 1, :] = gain_raw[pair * LANES : (pair + 1) * LANES].reshape(1, LANES)
+    for copy in small:
         copy.wait_recv()
+    sd_all[me] = sd_out[me].astype(F32)
+    for off in range(1, n_grp):
+        sd_all[lax.rem(me + n_grp - off, n_grp)] = sd_in[off].astype(F32)
     for q in range(n_grp):
-        b_blk = bc_all[q, :, :LANES]
-        c_blk = bc_all[q, :, LANES:]
-        b_t[q] = jnp.transpose(b_blk.astype(F32))
+        b_t[q] = jnp.transpose(b_all[q].astype(F32))
         both = lax.dot_general(
-            c_blk, b_blk, (((1,), (1,)), ((), ())), preferred_element_type=F32
+            c_all[q], b_all[q], (((1,), (1,)), ((), ())), preferred_element_type=F32
         )
         scores[q] = jnp.where(causal, both, 0.0)
         sums = dot(sd_all[q, 1].astype(BF16), after_ones)
         tail_w[q] = jnp.exp(sums[:, :LANES]) * sd_all[q, 0]
         total_e[q] = jnp.exp(sums[:, LANES:])
-    for copy in early[2 * (n_grp - 1) :]:
-        copy.wait_recv()
+    product = total_e[0]
+    for q in range(1, n_grp):
+        product = product * total_e[q]
+    dec[...] = product
+    dec_copy = pltpu.make_async_remote_copy(
+        src_ref=dec,
+        dst_ref=dec_in,
+        send_sem=dec_sem.at[0],
+        recv_sem=dec_sem.at[1],
+        device_id={"ctx": mate},
+        device_id_type=MESH_ID,
+    )
+    dec_copy.start()
 
     first_row = first[:1]
 
     def lanes_of(pair):
         return pl.ds(pl.multiple_of(pair * LANES, LANES), LANES)
 
-    def state_pair(pair, carry):
+    def mate_hop(pair):
+        return pltpu.make_async_remote_copy(
+            src_ref=mate_out.at[pair],
+            dst_ref=mate_in.at[pair],
+            send_sem=mate_send.at[pair],
+            recv_sem=mate_recv.at[pair],
+            device_id={"ctx": mate},
+            device_id_type=MESH_ID,
+        )
+
+    def row_of(ref, pair):
+        return jnp.where(
+            first_row, ref[pl.ds(2 * pair, 1), :], ref[pl.ds(2 * pair + 1, 1), :]
+        )
+
+    def state_pair(pair):
         state = jnp.zeros((LANES, LANES), F32)
         decay = jnp.ones((1, LANES), F32)
         for q in range(n_grp):
@@ -201,10 +288,8 @@
             state = state * total + fresh
             decay = decay * total
         s_fin[pair] = state
-        d_start[n_grp, pl.ds(pair, 1), :] = decay
-        return carry
-
-    lax.fori_loop(0, pairs, state_pair, 0)
+        mate_out[pair] = state.astype(mate_out.dtype)
+        mate_hop(pair).start()
 
     def hop(pair):
         return pltpu.make_async_remote_copy(
@@ -212,28 +297,42 @@
             dst_ref=chain_in.at[pair],
             send_sem=chain_send.at[pair],
             recv_sem=chain_recv.at[pair],
-            device_id={"ctx": lax.rem(ctx + 1, n_ctx)},
+            device_id={"ctx": lax.rem(ctx + 2, n_ctx)},
             device_id_type=MESH_ID,
         )
 
     def chain_pair(pair):
-        @pl.when(ctx == 0)
+        @pl.when(pair == 0)
+        def _():
+            dec_copy.wait_recv()
+
+        @pl.when(outer == 0)
         def _():
             chain_in[pair] = jnp.zeros((LANES, LANES), chain_in.dtype)
 
-        @pl.when(ctx > 0)
+        mate_hop(pair).wait_recv()
+
+        @pl.when(outer > 0)
         def _():
             hop(pair).wait_recv()
 
-        @pl.when(ctx < n_ctx - 1)
+        prefix = chain_in[pair].astype(F32)
+        other = mate_in[pair].astype(F32)
+        own_d = row_of(dec, pair)
+        other_d = row_of(dec_in, pair)
+
+        @pl.when(outer < n_out - 1)
         def _():
-            total = chain_in[pair].astype(F32) * d_start[n_grp, pl.ds(pair, 1), :] + s_fin[pair]
-            chain_out[pair] = total.astype(chain_out.dtype)
+            mine = s_fin[pair]
+            total = jnp.where(inner_ctx == 0, other_d * mine + other, own_d * other + mine)
+            chain_out[pair] = (own_d * other_d * prefix + total).astype(chain_out.dtype)
             hop(pair).start()
+
+        arrived_all[pair] = jnp.where(inner_ctx == 0, prefix, other_d * prefix + other)
 
     def within_pair(pair):
         at = lanes_of(pair)
-        skip = skip_ref[:, at]
+        skip = jnp.where(first_row, skip_raw[2 * pair], skip_raw[2 * pair + 1])
         for q in range(n_grp):
             x = chan_all[q, :, at]
             d0 = jnp.where(causal, sd_all[q, 1, pl.ds(2 * pair, 1), :], 0.0).astype(BF16)
@@ -248,12 +347,29 @@
             y = dot(weights, jnp.concatenate([x * left, x * right], axis=0))
             y_acc[q, :, at] = y + skip * x.astype(F32)
 
-    lag = jnp.minimum(ctx, pairs)
+    lag = jnp.minimum(1 + 2 * outer, 2 * pairs - 1)
 
     def mixed(step, carry):
         @pl.when(step < pairs)
         def _():
-            within_pair(step)
+            @pl.when(lax.rem(step, part_pairs) == 0)
+            def _():
+                part = step // part_pairs
+
+                @pl.when(part == n_part - 1)
+                def _():
+                    for late in range(n_part):
+                        for off in range(1, n_grp):
+                            gate_part(late, off).start()
+
+                for off in range(1, n_grp):
+                    chan_part(part, off).wait_recv()
+
+            state_pair(step)
+
+        @pl.when((step >= pairs) & (step < 2 * pairs))
+        def _():
+            within_pair(step - pairs)
 
         @pl.when((step >= lag) & (step < lag + pairs))
         def _():
@@ -261,27 +377,31 @@
 
         return carry
 
-    lax.fori_loop(0, 2 * pairs, mixed, 0)
-
-    own[3].wait()
-    for copy in late:
-        copy.wait_recv()
-    own[4].wait()
-
-    ssq_copies = {}
+    lax.fori_loop(0, 3 * pairs, mixed, 0)
+
+    for copy in own[7:]:
+        copy.wait()
+
     for turn in range(1, n_chip + 1):
         chip_to = lax.rem(chip + turn, n_chip)
 
-        def gate_pair(pair, sums, chip_to=chip_to):
+        def gate_pair(pair, sums, chip_to=chip_to, turn=turn):
+            if turn == 1:
+
+                @pl.when(lax.rem(pair, part_pairs) == 0)
+                def _():
+                    for off in range(1, n_grp):
+                        gate_part(pair // part_pairs, off).wait_recv()
+
             at = lanes_of(pair)
-            arrived = chain_in[pair].astype(F32)
-            gain = gain_ref[:, at]
+            arrived = arrived_all[pair]
+            gain = gain_rows[pl.ds(pair, 1), :]
             res = []
             for c in range(2):
                 q = chip_to * 2 + c
                 state = s_start[q, pair] + d_start[q, pl.ds(pair, 1), :] * arrived
                 y = y_acc[q, :, at] + e_acc[q, :, at] * dot(
-                    bc_all[q, :, LANES:], state.astype(BF16)
+                    c_all[q], state.astype(BF16)
                 )
                 g = gate_all[q, :, at].astype(F32)
                 gated = y * (g / (1.0 + jnp.exp(-g)))
@@ -375,15 +495,29 @@
 
     lax.fori_loop(0, n_col, finish, 0)
 
-    for copy in early + late:
+    for copy in small + [dec_copy]:
         copy.wait_send()
+
+    def chan_done(part, carry):
+        for off in range(1, n_grp):
+            chan_part(part, off).wait_send()
+            gate_part(part, off).wait_send()
+        return carry
+
+    lax.fori_loop(0, n_part, chan_done, 0)
     for off in range(1, n_grp):
         peer = lax.rem(me + off, n_grp)
         push(
             ssq_out.at[peer], ssq_in.at[off], ssq_send.at[off], ssq_recv.at[off], peer
         ).wait_send()
 
-    @pl.when(ctx < n_ctx - 1)
+    def mate_done(pair, carry):
+        mate_hop(pair).wait_send()
+        return carry
+
+    lax.fori_loop(0, pairs, mate_done, 0)
+
+    @pl.when(outer < n_out - 1)
     def _():
         def done(pair, carry):
             hop(pair).wait_send()
@@ -412,39 +546,43 @@
     pairs = width // LANES
     n_chip = n_grp // 2
     n_col = model // COLS
-    bc = jnp.concatenate([b_proj, c_proj], axis=1)
-    sd = jnp.stack(
-        [
-            jnp.transpose(step_size.astype(F32)).reshape(n_grp, heads, tok),
-            jnp.transpose(log_decay.astype(F32)).reshape(n_grp, heads, tok),
-        ],
-        axis=1,
-    )
-    skip = jnp.repeat(skip_gain, HD).reshape(1, width)
-    gain = norm_gain.reshape(1, width)
-    hbm = pl.BlockSpec(memory_space=pl.ANY)
+    padded = -(-heads // 16) * 16
+    n_part = 5 if pairs % 5 == 0 else 1
+    hbm = pl.BlockSpec(memory_space=pltpu.HBM)
     vmem = pl.BlockSpec(memory_space=pltpu.VMEM)
     dma = pltpu.SemaphoreType.DMA
     return pl.pallas_call(
         functools.partial(layer_kernel, n_ctx, n_grp, inner),
         out_shape=jax.ShapeDtypeStruct((tok, model), BF16),
-        in_specs=[hbm, hbm, hbm, hbm, vmem, vmem, hbm],
+        in_specs=[hbm] * 9,
         out_specs=vmem,
         scratch_shapes=[
             pltpu.VMEM((n_grp, tok, width), BF16),
             pltpu.VMEM((n_grp, tok, width), BF16),
-            pltpu.VMEM((n_grp, tok, 2 * LANES), BF16),
-            pltpu.VMEM((n_grp, 2, heads, tok), F32),
+            pltpu.VMEM((n_grp * heads, tok), BF16),
+            pltpu.VMEM((n_grp * heads, tok), BF16),
+            pltpu.SMEM((heads,), F32),
+            pltpu.VMEM((width,), F32),
+            pltpu.VMEM((n_grp, tok, LANES), BF16),
+            pltpu.VMEM((n_grp, tok, LANES), BF16),
+            pltpu.VMEM((n_grp, 2, padded, tok), BF16),
+            pltpu.VMEM((n_grp, 2, padded, tok), BF16),
+            pltpu.VMEM((n_grp, 2, padded, tok), F32),
             pltpu.VMEM((width, model), BF16),
             pltpu.VMEM((n_grp, LANES, tok), F32),
             pltpu.VMEM((n_grp, tok, tok), F32),
-            pltpu.VMEM((n_grp, heads, LANES), F32),
-            pltpu.VMEM((n_grp, heads, LANES), F32),
+            pltpu.VMEM((n_grp, padded, LANES), F32),
+            pltpu.VMEM((n_grp, padded, LANES), F32),
             pltpu.VMEM((n_grp, tok, width), F32),
             pltpu.VMEM((n_grp, tok, width), F32),
             pltpu.VMEM((n_chip, 2 * tok, width), BF16),
             pltpu.VMEM((n_grp, pairs, LANES, LANES), F32),
-            pltpu.VMEM((n_grp + 1, pairs, LANES), F32),
+            pltpu.VMEM((n_grp, pairs, LANES), F32),
+            pltpu.VMEM((pairs, LANES, LANES), F32),
+            pltpu.VMEM((padded, LANES), F32),
+            pltpu.VMEM((padded, LANES), F32),
+            pltpu.VMEM((pairs, LANES, LANES), BF16),
+            pltpu.VMEM((pairs, LANES, LANES), BF16),
             pltpu.VMEM((pairs, LANES, LANES), F32),
             pltpu.VMEM((pairs, LANES, LANES), BF16),
             pltpu.VMEM((pairs, LANES, LANES), BF16),
@@ -454,17 +592,23 @@
             pltpu.VMEM((n_chip - 1, n_col, tok, COLS), BF16),
             pltpu.VMEM((n_chip - 1, n_col, tok, COLS), BF16),
             pltpu.VMEM((n_col, tok, COLS), F32),
+            pltpu.VMEM((pairs, LANES), F32),
             pltpu.VMEM((n_grp, 8, tok), F32),
             pltpu.VMEM((n_grp, 8, tok), F32),
-            dma((5,)),
-            dma((n_grp,)),
-            dma((n_grp,)),
-            dma((n_grp,)),
-            dma((n_grp,)),
-            dma((n_grp,)),
-            dma((n_grp,)),
-            dma((n_grp,)),
-            dma((n_grp,)),
+            dma((9,)),
+            dma((n_part, n_grp)),
+            dma((n_part, n_grp)),
+            dma((n_part, n_grp)),
+            dma((n_part, n_grp)),
+            dma((n_grp,)),
+            dma((n_grp,)),
+            dma((n_grp,)),
+            dma((n_grp,)),
+            dma((n_grp,)),
+            dma((n_grp,)),
+            dma((2,)),
+            dma((pairs,)),
+            dma((pairs,)),
             dma((pairs,)),
             dma((pairs,)),
             dma((n_chip, n_col)),
@@ -475,10 +619,20 @@
             dma((n_grp,)),
         ],
         compiler_params=pltpu.CompilerParams(
-            collective_id=0, has_side_effects=True, vmem_limit_bytes=52 << 20
+            collective_id=0, has_side_effects=True, vmem_limit_bytes=64 << 20
         ),
         name="layer",
-    )(channels, gates, bc, sd, skip, gain, out_weight)
+    )(
+        channels,
+        gates,
+        b_proj,
+        c_proj,
+        jnp.transpose(step_size),
+        jnp.transpose(log_decay),
+        skip_gain,
+        norm_gain,
+        out_weight,
+    )
 
 
 def solution(mesh):

time: 72 us -> 63.2 us (0.88)
  the two profiles are of different devices: /device:TPU:30 before, /device:TPU:0 now
where the time goes in v2:
time: 63.2 us; the launch traced here: 63 us
  Pallas kernels  61 us (97%)
  local copies, waits for them, and re-layouts  1.97 us (3%)
    pallas_call x1, Pallas kernels, local(): pl.pallas_call(functools.partial(layer_kernel, n_ctx, n_grp, inner), out_...  61 us
    unnamed x1, local copies, waits for them, and re-layouts  1.97 us

profile of v2, /device:TPU:0, one launch (start us, length us, event | category | flops | bytes accessed | tf_op | source)
XLA Modules:
  0.0 63.0 jit_solution(2537253822745463964)
XLA Ops:
  0.0 61.0 %layer.1 = bf16[128,2560]{1,0:T(8,128)(2,1)} custom-call(bf16[128,5120]{1,0:T(8,128)(2,1)} %chan_ref.1, bf16[128,5120]{1,0:T(8,128)(2,1)} %gate_ref.1, bf16[128,128]{1,0:T(8,128)(2,1)} %b_ref.1, bf16[128,128]{1,0:T(8,128)(2,1)} %c_ref.1, bf16[80,128]{1,0:T(8,128)(2,1)} %bitcast.2, bf16[80,128]{1,0:T(8,128)(2,1)} %bitcast.3, f32[20]{0:T(128)} %skip_ref.1, ...), custom_call_target="tpu_custom_call" | custom-call | tf_op jit(solution)/shard_map/layer/pallas_call | solution.py:554
  61.0 2.0 %copy.11 = bf16[128,2560]{1,0:T(8,128)(2,1)} copy(bf16[128,2560]{1,0:T(8,128)(2,1)} %layer.1) | data formatting | bytes 1310720

commit v3 on v2

--- a/solution.py
+++ b/solution.py
@@ -347,7 +347,7 @@
             y = dot(weights, jnp.concatenate([x * left, x * right], axis=0))
             y_acc[q, :, at] = y + skip * x.astype(F32)
 
-    lag = jnp.minimum(1 + 2 * outer, 2 * pairs - 1)
+    lag = jnp.minimum(2 + 3 * outer, 2 * pairs - 1)
 
     def mixed(step, carry):
         @pl.when(step < pairs)

time: 63.2 us -> 60.2 us (0.953)
  Pallas kernels: 61 us -> 58 us
    pallas_call x1, Pallas kernels: 61 us -> 58 us  [local(): pl.pallas_call(functools.partial(layer_kernel, n_ctx, n_grp, inner), out_...]
where the time goes in v3:
time: 60.2 us; the launch traced here: 60 us
  Pallas kernels  58 us (96%)
  local copies, waits for them, and re-layouts  1.97 us (3%)
    pallas_call x1, Pallas kernels, local(): pl.pallas_call(functools.partial(layer_kernel, n_ctx, n_grp, inner), out_...  58 us
    unnamed x1, local copies, waits for them, and re-layouts  1.97 us

profile of v3, /device:TPU:0, one launch (start us, length us, event | category | flops | bytes accessed | tf_op | source)
XLA Modules:
  0.0 60.0 jit_solution(16736907768869552148)
XLA Ops:
  0.0 58.0 %layer.1 = bf16[128,2560]{1,0:T(8,128)(2,1)} custom-call(bf16[128,5120]{1,0:T(8,128)(2,1)} %chan_ref.1, bf16[128,5120]{1,0:T(8,128)(2,1)} %gate_ref.1, bf16[128,128]{1,0:T(8,128)(2,1)} %b_ref.1, bf16[128,128]{1,0:T(8,128)(2,1)} %c_ref.1, bf16[80,128]{1,0:T(8,128)(2,1)} %bitcast.2, bf16[80,128]{1,0:T(8,128)(2,1)} %bitcast.3, f32[20]{0:T(128)} %skip_ref.1, ...), custom_call_target="tpu_custom_call" | custom-call | tf_op jit(solution)/shard_map/layer/pallas_call | solution.py:554
  58.0 2.0 %copy.11 = bf16[128,2560]{1,0:T(8,128)(2,1)} copy(bf16[128,2560]{1,0:T(8,128)(2,1)} %layer.1) | data formatting | bytes 1310720
